TPU v7x, 128 devices: a whole 4x4x4 slice. The times are simulated.
128 devices in a mesh: group: 8 (over x, core), member: 16 (over z, y).
Axes of the slice: x: 4, y: 4, z: 4, core: 2. Of those that a mesh axis runs over, the one named last changes fastest.
Arguments:
- embeddings: float32 [65536, 768], P(('group', 'member'))
- cluster: int32 [65536], P(('group', 'member')), may hold values from 0 to 63, as said below
- slot: int32 [65536], P(('group', 'member')), may hold values from 0 to 1023, as said below
Outputs:
- dup_score: float32 [65536], P(('group', 'member'))
Inputs may be any that keep to these rules, and one draw needn't show every extreme that they name: The 512 documents of one device name distinct slots; slot // 8 is the receiving device in group-major order; in every draw one receiving device gets all 8 of its slots filled from every device. All documents of one cluster name slots of devices of one group; in each group one of its 8 clusters holds most of the group's documents.
All inputs are finite; a program needn't handle non-finite values.
Results may differ from a plain program's by a relative error of at most 0.0012.
Values may be sent and summed in bfloat16 or wider, within the bound.
A program may use at most 128 MiB of HBM per device.

v0:
```python
import jax
import jax.numpy as jnp
from jax import lax
from jax.sharding import PartitionSpec as P


def unit_rows(values):
    return (values * lax.rsqrt(jnp.sum(values * values, axis=1, keepdims=True) + 1e-06)).astype(
        jnp.bfloat16
    )


def tile_terms(queries, query_labels, keys, key_labels, query_pos, key_pos):
    cosine = jnp.einsum("qd,kd->qk", queries, keys, preferred_element_type=jnp.float32)
    same = (query_labels[:, None] == key_labels[None, :]) & (key_labels[None, :] >= 0)
    same = same & (query_pos[:, None] != key_pos[None, :])
    return jnp.where(same, jnp.exp(20.0 * (cosine - 1.0)), jnp.float32(0.0))


def body(embeddings, cluster, slot):
    rows = embeddings.shape[0]
    width = embeddings.shape[1]
    slots_dev = 2 * rows
    unit = unit_rows(embeddings)
    send_rows = jnp.zeros((slots_dev, width), jnp.bfloat16).at[slot].set(unit)
    send_labels = jnp.full((slots_dev,), -1, jnp.int32).at[slot].set(cluster)
    got_rows, got_labels = (
        lax.all_to_all(send_rows, ("group", "member"), split_axis=0, concat_axis=0, tiled=True),
        lax.all_to_all(send_labels, ("group", "member"), split_axis=0, concat_axis=0, tiled=True),
    )
    member_index = lax.axis_index("member")
    query_pos = member_index * slots_dev + jnp.arange(slots_dev, dtype=jnp.int32)
    keys = lax.all_gather(got_rows, "member", axis=0, tiled=True)
    key_labels = lax.all_gather(got_labels, "member", axis=0, tiled=True)
    key_pos = jnp.arange(keys.shape[0], dtype=jnp.int32)
    terms = tile_terms(got_rows, got_labels, keys, key_labels, query_pos, key_pos)
    totals = jnp.sum(terms, axis=1)
    scores = jnp.log(1.0 + totals)
    back = lax.all_to_all(scores, ("group", "member"), split_axis=0, concat_axis=0, tiled=True)
    return back[slot]


def solution(mesh):
    in_specs = (P(("group", "member"), None), P(("group", "member")), P(("group", "member")))
    out_specs = P(("group", "member"))
    return jax.shard_map(body, mesh=mesh, in_specs=in_specs, out_specs=out_specs, check_vma=False)
```

profile of v0, /device:TPU:1, one launch (start us, length us, event | category | flops | bytes accessed | tf_op | source)
XLA Modules:
  0.0 274.4 jit_solution(12988017705148283308)
XLA Ops:
  6.5 0.0 all-gather.2.cloned.1.call-start
  6.5 0.7 compare_select_fusion
  7.2 1.6 multiply_reduce_fusion
  8.8 3.9 %scatter_custom_fusion.1 = bf16[1024,768]{1,0:T(8,128)(2,1)S(1)} fusion(s32[512]{0:T(512)S(1)} %compare_select_fusion, f32[512,768]{1,0:T(8,128)} %param.3, f32[512]{0:T(512)S(1)} %add_rsqrt_fusion, bf16[]{:T(256)} %constant.3.clone.1), kind=kCustom, calls=%fused_computation.8 | custom fusion | flops 786432 | bytes 3147778 | tf_op jit(solution)/shard_map/scatter | solution.py:25
  12.7 35.5 %all_to_all.30 = bf16[128,8,768]{2,1,0:T(8,128)(2,1)} all-to-all(bf16[128,8,768]{2,1,0:T(8,128)(2,1)S(1)} %bitcast.10), channel_id=1, replica_groups=mesh['group'=8,'member'=16] {'group','member'}, dimensions={0} | all-to-all | bytes 3145728 | tf_op jit(solution)/shard_map/all_to_all | solution.py:28
  48.2 0.0 all-gather.2.cloned.1.call-update
  48.2 2.6 scatter_custom_fusion
  50.9 0.7 all_to_all.20
  51.6 4.8 %all-to-all-start = ((s32[128,8,1]{1,2,0:T(1,128)}), s32[128,8,1]{1,2,0:T(1,128)S(1)}, u32[]{:S(2)}, u32[]{:S(2)}) async-start(s32[128,8,1]{1,2,0:T(1,128)} %bitcast), calls=%async_computation | async-start | bytes 131072 | tf_op jit(solution)/shard_map/all_to_all | solution.py:29
  56.3 9.9 %all-to-all-done = s32[128,8,1]{1,2,0:T(1,128)S(1)} async-done(((s32[128,8,1]{1,2,0:T(1,128)}), s32[128,8,1]{1,2,0:T(1,128)S(1)}, u32[]{:S(2)}, u32[]{:S(2)}) %all-to-all-start) | async-done | bytes 4128 | tf_op jit(solution)/shard_map/all_to_all | solution.py:29
  66.2 0.5 broadcast.46
  66.7 0.8 reduce.6
  67.6 0.1 eq.15
  67.7 18.5 %all_gather.6 = s32[16384]{0:T(1024)S(1)} all-gather(s32[1024]{0:T(1024)S(1)} %eq.15), channel_id=1, replica_groups=mesh['group'=8,'member'=16] {'member'}, dimensions={0}, use_global_device_ids=true | all-gather | bytes 69632 | tf_op jit(solution)/shard_map/all_gather | solution.py:34
  86.2 113.8 %all-gather.2.cloned.1.call-done = bf16[16384,768]{1,0:T(8,128)(2,1)} async-done(((bf16[1024,768]{1,0:T(8,128)(2,1)}), bf16[16384,768]{1,0:T(8,128)(2,1)}) %all-gather.2.cloned.1.call-update) | async-done | bytes 25165840 | tf_op jit(solution)/shard_map/all_gather | solution.py:33
  200.0 44.4 %select_reduce_fusion = f32[1024]{0:T(1024)S(1)} fusion(s32[1024]{0:T(1024)S(1)} %iota_add_fusion, s32[16384]{0:T(1024)S(1)} %all_gather.6, s32[1024]{0:T(1024)S(1)} %eq.15, pred[16384]{0:T(1024)(128)(4,1)S(1)} %broadcast_compare_fusion, bf16[16384,768]{1,0:T(8,128)(2,1)} %all-gather.2.cloned.1.call-done, bf16[128,8,768]{2,1,0:T(8,128)(2,1)} %all_to_all.30), kind=kOutput, calls=%fused_computation.3 | convolution fusion | flops 25904021504 | bytes 26832896 | tf_op jit(solution)/shard_map/qd,kd->qk/dot_general | solution.py:14
  244.3 0.7 log.14
  245.1 7.9 %all-to-all-start.2 = ((f32[128,8,1]{1,2,0:T(1,128)}), f32[128,8,1]{1,2,0:T(1,128)S(1)}, u32[]{:S(2)}, u32[]{:S(2)}) async-start(f32[128,8,1]{1,2,0:T(1,128)} %bitcast.3), calls=%async_computation.2 | async-start | bytes 131072 | tf_op jit(solution)/shard_map/all_to_all | solution.py:39
  253.0 9.8 %all-to-all-done.2 = f32[128,8,1]{1,2,0:T(1,128)S(1)} async-done(((f32[128,8,1]{1,2,0:T(1,128)}), f32[128,8,1]{1,2,0:T(1,128)S(1)}, u32[]{:S(2)}, u32[]{:S(2)}) %all-to-all-start.2) | async-done | bytes 4128 | tf_op jit(solution)/shard_map/all_to_all | solution.py:39
  262.7 0.5 broadcast.47
  263.3 0.8 reduce.7
  264.1 0.1 all_to_all.26
  264.2 3.4 %gather_fusion = f32[512]{0:T(512)} fusion(f32[1024]{0:T(1024)S(1)} %all_to_all.26, s32[1024]{0:T(1024)S(1)} %pad_clamp_fusion), kind=kCustom, calls=%fused_computation | custom fusion | bytes 6144 | tf_op jit(solution)/shard_map/gather | solution.py:40
  (5 shorter events, 0.0 us)
Async XLA Ops:
  6.5 193.4 %all-gather.2.cloned.1.call-start = ((), (), s32[]{:S(2)}) async-start(), calls=%async_computation.3 | async-start | bytes 26738688 | tf_op jit(solution)/shard_map/all_gather | solution.py:33
  51.6 14.7 %all-to-all-start = ((s32[128,8,1]{1,2,0:T(1,128)}), s32[128,8,1]{1,2,0:T(1,128)S(1)}, u32[]{:S(2)}, u32[]{:S(2)}) async-start(s32[128,8,1]{1,2,0:T(1,128)} %bitcast), calls=%async_computation | async-start | bytes 131072 | tf_op jit(solution)/shard_map/all_to_all | solution.py:29
  245.1 17.7 %all-to-all-start.2 = ((f32[128,8,1]{1,2,0:T(1,128)}), f32[128,8,1]{1,2,0:T(1,128)S(1)}, u32[]{:S(2)}, u32[]{:S(2)}) async-start(f32[128,8,1]{1,2,0:T(1,128)} %bitcast.3), calls=%async_computation.2 | async-start | bytes 131072 | tf_op jit(solution)/shard_map/all_to_all | solution.py:39
Sparse Core Ops, SparseCore 0:
  48.4 151.5 all-gather.1
where the time goes:
time: 275 us; the launch traced here: 274 us
  waiting for transfers between devices  133 us (48%)
  blocking collectives  54 us (20%)
  matrix products  44.4 us (16%)
  between operations  13.5 us (5%)
  starting transfers between devices  12.7 us (5%)
  local copies, waits for them, and re-layouts  8.63 us (3%)
  other arithmetic  7.81 us (3%)
    all_gather x1, waiting for transfers between devices, body(): keys = lax.all_gather(got_rows, 'member', axis=0, tiled=True)  114 us
    dot_general x1, matrix products, tile_terms(): jnp.einsum('qd,kd->qk', queries, keys, preferred_element_type=jnp.float32)  44.4 us
    all_to_all x1, blocking collectives, body(): lax.all_to_all(send_rows, ('group', 'member'), split_axis=0, concat_axis=...  35.5 us
    all_gather x1, blocking collectives, body(): key_labels = lax.all_gather(got_labels, 'member', axis=0, tiled=True)  18.5 us
    all_to_all x1, waiting for transfers between devices, body(): lax.all_to_all(send_labels, ('group', 'member'), split_axis=0, concat_axi...  9.9 us
    all_to_all x1, waiting for transfers between devices, body(): lax.all_to_all(scores, ('group', 'member'), split_axis=0, concat_axis=0,...  9.77 us
    all_to_all x1, starting transfers between devices, body(): lax.all_to_all(scores, ('group', 'member'), split_axis=0, concat_axis=0,...  7.9 us
  transfers between devices with their start and end apart: 3, of which 3 were waited for; matrix products, arithmetic and copies ran while one was open for 1% of the time, Pallas kernels for 0%

commit v1 on v0

v1 whole, which is shorter than its diff:
```python
import functools
import math

import jax
import jax.numpy as jnp
from jax import lax
from jax.experimental import pallas as pl
from jax.experimental.pallas import tpu as pltpu
from jax.sharding import PartitionSpec as P

D = 768
CAPB = 96
DOCS = CAPB - 1
NQ = 8
BLK = NQ * CAPB
ND = 6
FLAG_LANE = 127
SCALE = 20.0 * math.log2(math.e)
MESH = pl.DeviceIdType.MESH
HELD = ((0, 0), (1, 0), (3, 0), (2, 0), (0, 1), (0, 2))
PAIRS = (
    (0, 0, False),
    (0, 1, True),
    (0, 3, False),
    (0, 4, True),
    (1, 4, True),
    (2, 4, True),
    (3, 4, True),
    (0, 5, False),
    (1, 5, True),
    (3, 5, False),
)
ORDER = (0, 1, 2, 3, 6, 7, 4, 5)


def pack_kernel(emb_ref, slot_ref, clu_ref, send_ref, meta_ref):
    rows = emb_ref.shape[0]
    slot = slot_ref[...]
    group = slot // 128
    ids = lax.broadcasted_iota(jnp.int32, (8, rows), 0)
    member = (ids == group).astype(jnp.float32)
    upper = lax.broadcasted_iota(jnp.int32, (rows, rows), 0) < lax.broadcasted_iota(
        jnp.int32, (rows, rows), 1
    )
    before = jnp.dot(
        member.astype(jnp.bfloat16),
        upper.astype(jnp.float32).astype(jnp.bfloat16),
        preferred_element_type=jnp.float32,
    )
    rank = jnp.sum(member * before, axis=0, keepdims=True).astype(jnp.int32)
    fits = rank < DOCS
    overflow = jnp.max(jnp.where(fits, 0.0, 1.0))
    place = jnp.where(fits, group * CAPB + rank, -1)
    meta_ref[0:1, :] = group
    meta_ref[1:2, :] = rank

    values = emb_ref[...]
    squares = jnp.sum(values * values, axis=1, keepdims=True)
    unit = (values * lax.rsqrt(squares + 1e-06)).astype(jnp.bfloat16)

    lane = lax.broadcasted_iota(jnp.int32, (128, rows), 0)
    at_rank = ((lane == rank) & fits).astype(jnp.float32).astype(jnp.bfloat16)
    label = (member * (clu_ref[...] + 1).astype(jnp.float32)).astype(jnp.bfloat16)
    labels = lax.dot_general(
        label, at_rank, (((1,), (1,)), ((), ())), preferred_element_type=jnp.float32
    )
    lanes = lax.broadcasted_iota(jnp.int32, (8, 128), 1)
    labels = jnp.where(lanes == FLAG_LANE, overflow, labels)
    row = lax.broadcasted_iota(jnp.int32, (CAPB, rows), 0)
    last = lax.broadcasted_iota(jnp.int32, (CAPB, 128), 0) == DOCS
    for g in range(8):
        chosen = (row + g * CAPB == place).astype(jnp.float32).astype(jnp.bfloat16)
        packed = jnp.dot(chosen, unit, preferred_element_type=jnp.float32)
        head = jnp.where(last, labels[g : g + 1, :], packed[:, :128])
        send_ref[g, :, :128] = head.astype(jnp.bfloat16)
        send_ref[g, :, 128:] = packed[:, 128:].astype(jnp.bfloat16)


def pack(embeddings, slot, cluster):
    rows = embeddings.shape[0]
    return pl.pallas_call(
        pack_kernel,
        out_shape=(
            jax.ShapeDtypeStruct((8, CAPB, D), jnp.bfloat16),
            jax.ShapeDtypeStruct((2, rows), jnp.int32),
        ),
        in_specs=[pl.BlockSpec(memory_space=pltpu.VMEM)] * 3,
        out_specs=(pl.BlockSpec(memory_space=pltpu.VMEM),) * 2,
        compiler_params=pltpu.CompilerParams(vmem_limit_bytes=24 << 20),
        name="pack",
    )(embeddings, slot.reshape(1, rows), cluster.reshape(1, rows))


def score_kernel(
    send_ref,
    got_ref,
    blk,
    relay,
    lrow,
    lcol,
    rsum,
    csum,
    ret,
    own_sem,
    arr_sem,
    out_sem,
    rel_in,
    rel_out,
    p1_out,
    ret_in,
    ret_out,
):
    gi = lax.axis_index("group")
    mi = lax.axis_index("member")
    x, c = gi // 2, gi % 2
    z, y = mi // 4, mi % 4

    def line_coord(t):
        return x * (1 - t) + z * t

    def line_dev(t, off, core):
        return (((x + (1 - t) * off) % 4) * 2 + core, ((z + t * off) % 4) * 4 + y)

    def plane_dev(a, b):
        px = (x + c * a) % 4
        pz = (z + (1 - c) * a) % 4
        py = (y + b * (1 + 2 * c)) % 4
        return (px * 2 + c, pz * 4 + py)

    def remote(src, dst, send_sem, recv_sem, dev):
        return pltpu.make_async_remote_copy(
            src_ref=src,
            dst_ref=dst,
            send_sem=send_sem,
            recv_sem=recv_sem,
            device_id=dev,
            device_id_type=MESH,
        )

    def chunk(m, q):
        return blk.at[m, pl.ds(q * CAPB, CAPB), :]

    own = pltpu.make_async_copy(send_ref.at[2 * line_coord(c) + c], chunk(0, 0), own_sem)
    own.start()

    barrier = pltpu.get_barrier_semaphore()
    partners = [
        (x * 2 + 1 - c, mi),
        line_dev(c, 1, c),
        line_dev(c, 3, c),
        line_dev(1 - c, 1, 1 - c),
        line_dev(1 - c, 3, 1 - c),
        line_dev(c, 1, 1 - c),
        line_dev(c, 3, 1 - c),
        plane_dev(1, 0),
        plane_dev(3, 0),
        plane_dev(0, 1),
        plane_dev(0, 3),
    ]
    for dev in partners:
        pl.semaphore_signal(barrier, inc=1, device_id=dev, device_id_type=MESH)
    pl.semaphore_wait(barrier, len(partners))

    sent = []

    def start(copy):
        copy.start()
        sent.append(copy)

    for tau in (1, 0):
        t = c if tau == 0 else 1 - c
        at = line_coord(t)
        step = 1 if tau == 0 else 3
        if tau == 1:
            start(
                remote(
                    send_ref.at[2 * at + t], chunk(0, 1), p1_out.at[0], arr_sem.at[1],
                    (x * 2 + t, mi),
                )
            )
        start(
            remote(
                send_ref.at[2 * ((at + 2) % 4) + t], relay.at[tau], p1_out.at[1 + tau],
                rel_in.at[tau], line_dev(t, step, c),
            )
        )
    for off, q in ((1, 6), (3, 2)):
        for tau in (0, 1):
            t = c if tau == 0 else 1 - c
            at = line_coord(t)
            start(
                remote(
                    send_ref.at[2 * ((at + off) % 4) + t], chunk(0, q + tau),
                    p1_out.at[3 + tau + (0 if off == 1 else 2)], arr_sem.at[q + tau],
                    line_dev(t, off, t),
                )
            )

    def arrived(m, q):
        pltpu.make_async_copy(chunk(m, q), chunk(m, q), arr_sem.at[m * NQ + q]).wait()

    def pass_on(m, src, q, dev):
        start(
            remote(
                chunk(src, q), chunk(m, q), out_sem.at[(m - 1) * NQ + q],
                arr_sem.at[m * NQ + q], dev,
            )
        )

    for k in range(NQ + 1):
        if k == 2:
            for tau in (0, 1):
                t = c if tau == 0 else 1 - c
                pltpu.make_async_copy(relay.at[tau], relay.at[tau], rel_in.at[tau]).wait()
                start(
                    remote(
                        relay.at[tau], chunk(0, 4 + tau), rel_out.at[tau],
                        arr_sem.at[4 + tau], line_dev(t, 1 if tau == 0 else 3, t),
                    )
                )
        if k < NQ:
            q = ORDER[k]
            if q == 0:
                own.wait()
            else:
                arrived(0, q)
            pass_on(4, 0, q, plane_dev(0, 1))
            pass_on(1, 0, q, plane_dev(1, 0))
            pass_on(2, 0, q, plane_dev(3, 0))
        if k >= 1:
            q = ORDER[k - 1]
            arrived(4, q)
            pass_on(5, 4, q, plane_dev(0, 1))
            arrived(1, q)
            if k % 2 == 0:
                pass_on(3, 1, q, plane_dev(1, 0))
            arrived(2, q)
            if k % 2 == 1:
                pass_on(3, 2, q, plane_dev(3, 0))
    for k in range(NQ):
        arrived(3, ORDER[k])
        arrived(5, ORDER[k])

    lanes = lax.broadcasted_iota(jnp.int32, (1, 128), 1)
    overflow = jnp.zeros((1, 128), jnp.float32)
    for m in range(ND):
        rows = []
        for q in range(NQ):
            tail = blk[m, pl.ds(q * CAPB + CAPB - 16, 16), 0:128].astype(jnp.float32)
            rows.append(tail[15:16, :])
        labels = jnp.concatenate(rows, axis=0)
        overflow = jnp.maximum(overflow, jnp.max(labels, axis=0, keepdims=True))
        labels = jnp.where(lanes < DOCS, labels, 0.0)
        wide = jnp.zeros((8, BLK), jnp.float32)
        for q in range(NQ):
            piece = jnp.concatenate(
                [jnp.broadcast_to(labels[q : q + 1, :], (8, 128)), jnp.zeros((8, BLK - 128), jnp.float32)],
                axis=1,
            )
            wide = wide + (pltpu.roll(piece, q * CAPB, axis=1) if q else piece)
        lrow[m] = wide
        full = jnp.concatenate([labels, jnp.zeros((120, 128), jnp.float32)], axis=0)
        turned = jnp.transpose(full)
        for q in range(NQ):
            column = jnp.broadcast_to(turned[0:CAPB, q : q + 1], (CAPB, 128))
            lcol[m, pl.ds(q * CAPB, CAPB), :] = jnp.where(column == 0.0, -1.0, column)

    rsum[...] = jnp.zeros_like(rsum)
    csum[...] = jnp.zeros_like(csum)
    tile = 256
    for i, j, both in PAIRS:

        @pl.loop(0, BLK // tile)
        def _(r):
            at = pl.multiple_of(r * tile, tile)
            cosine = lax.dot_general(
                blk[i, pl.ds(at, tile), :],
                blk[j],
                (((1,), (1,)), ((), ())),
                preferred_element_type=jnp.float32,
            )
            column = lcol[i, pl.ds(at, tile), :]
            total = jnp.zeros((tile, 128), jnp.float32)
            for n in range(BLK // 128):
                part = cosine[:, n * 128 : (n + 1) * 128]
                same = column == lrow[j, 0:1, n * 128 : (n + 1) * 128]
                if i == j:
                    here = at + lax.broadcasted_iota(jnp.int32, (tile, 128), 0)
                    there = n * 128 + lax.broadcasted_iota(jnp.int32, (tile, 128), 1)
                    same = same & (here != there)
                term = jnp.where(same, jnp.exp2(part * SCALE - SCALE), 0.0)
                total = total + term
                if both:
                    csum[j, :, n * 128 : (n + 1) * 128] += jnp.sum(
                        term.reshape(tile // 8, 8, 128), axis=0
                    )
            rsum[i, pl.ds(at, tile), :] += total

    flag = jnp.max(jnp.where(lanes == FLAG_LANE, overflow, 0.0))
    for m in range(ND):
        line = jnp.sum(csum[m], axis=0, keepdims=True)
        if m < 4:
            line = line + jnp.sum(jnp.transpose(rsum[m]), axis=0, keepdims=True)
        line = jnp.broadcast_to(line, (8, BLK))
        for q in range(NQ):
            piece = (pltpu.roll(line, BLK - q * CAPB, axis=1) if q else line)[0:1, 0:128]
            ret[m, q] = jnp.where(lanes == FLAG_LANE, flag, piece)
    group = 2 * line_coord(c) + c
    for m in range(ND):
        a, b = HELD[m]
        for q in range(NQ):
            if m == 0 and q == 0:
                pltpu.make_async_copy(ret.at[0, 0], got_ref.at[0, group], ret_in).start()
                continue
            dl, cs = q // 2, q % 2
            core = c if cs == 0 else 1 - c
            px = (x + c * (4 - a) + (1 - c) * dl) % 4
            pz = (z + (1 - c) * (4 - a) + c * dl) % 4
            py = (y + (4 - b) * (1 + 2 * c)) % 4
            remote(
                ret.at[m, q], got_ref.at[m, group], ret_out, ret_in, (px * 2 + core, pz * 4 + py)
            ).start()
    pltpu.make_async_copy(got_ref, got_ref, ret_in).wait()
    for copy in sent:
        copy.wait_send()
    most = ret.at[0, pl.ds(1, NQ - 1)]
    pltpu.make_async_copy(most, most, ret_out).wait()
    rest = ret.at[pl.ds(1, ND - 1)]
    pltpu.make_async_copy(rest, rest, ret_out).wait()


def partial_sums(send):
    dma = pltpu.SemaphoreType.DMA
    return pl.pallas_call(
        score_kernel,
        out_shape=jax.ShapeDtypeStruct((ND, 8, 1, 128), jnp.float32),
        in_specs=[pl.BlockSpec(memory_space=pltpu.VMEM)],
        out_specs=pl.BlockSpec(memory_space=pltpu.VMEM),
        scratch_shapes=[
            pltpu.VMEM((ND, BLK, D), jnp.bfloat16),
            pltpu.VMEM((2, CAPB, D), jnp.bfloat16),
            pltpu.VMEM((ND, 8, BLK), jnp.float32),
            pltpu.VMEM((ND, BLK, 128), jnp.float32),
            pltpu.VMEM((4, BLK, 128), jnp.float32),
            pltpu.VMEM((ND, 8, BLK), jnp.float32),
            pltpu.VMEM((ND, NQ, 1, 128), jnp.float32),
            dma(()),
            dma((ND * NQ,)),
            dma(((ND - 1) * NQ,)),
            dma((2,)),
            dma((2,)),
            dma((7,)),
            dma(()),
            dma(()),
        ],
        compiler_params=pltpu.CompilerParams(
            collective_id=0, has_side_effects=True, vmem_limit_bytes=48 << 20
        ),
        name="scores",
    )(send)


def pick_kernel(got_ref, meta_ref, out_ref, flag_ref):
    total = got_ref[0, :, 0, :]
    for m in range(1, ND):
        total = total + got_ref[m, :, 0, :]
    lanes = lax.broadcasted_iota(jnp.int32, (8, 128), 1)
    flag_ref[...] = jnp.max(jnp.where(lanes == FLAG_LANE, total, 0.0), keepdims=True)
    scores = jnp.log(1.0 + total)
    ids = lax.broadcasted_iota(jnp.int32, (8, 128), 0)
    for n in range(out_ref.shape[1] // 128):
        group = meta_ref[0:1, n * 128 : (n + 1) * 128]
        rank = jnp.broadcast_to(meta_ref[1:2, n * 128 : (n + 1) * 128], (8, 128))
        values = jnp.take_along_axis(scores, jnp.minimum(rank, 127), axis=1)
        out_ref[:, n * 128 : (n + 1) * 128] = jnp.sum(
            jnp.where(ids == group, values, 0.0), axis=0, keepdims=True
        )


def pick(got, meta):
    rows = meta.shape[1]
    return pl.pallas_call(
        pick_kernel,
        out_shape=(
            jax.ShapeDtypeStruct((1, rows), jnp.float32),
            jax.ShapeDtypeStruct((1, 1), jnp.float32),
        ),
        in_specs=[pl.BlockSpec(memory_space=pltpu.VMEM)] * 2,
        out_specs=(pl.BlockSpec(memory_space=pltpu.VMEM),) * 2,
        name="pick",
    )(got, meta)


def general(embeddings, cluster, slot):
    rows, width = embeddings.shape
    slots_dev = 2 * rows
    unit = (
        embeddings * lax.rsqrt(jnp.sum(embeddings * embeddings, axis=1, keepdims=True) + 1e-06)
    ).astype(jnp.bfloat16)
    both = ("group", "member")
    send_rows = jnp.zeros((slots_dev, width), jnp.bfloat16).at[slot].set(unit)
    send_labels = jnp.full((slots_dev,), -1, jnp.int32).at[slot].set(cluster)
    got_rows = lax.all_to_all(send_rows, both, split_axis=0, concat_axis=0, tiled=True)
    got_labels = lax.all_to_all(send_labels, both, split_axis=0, concat_axis=0, tiled=True)
    members = lax.axis_size("member")
    ring = [(i, (i + 1) % members) for i in range(members)]
    index = jnp.arange(slots_dev, dtype=jnp.int32)

    def step(turn, state):
        keys, labels, totals = state
        cosine = jnp.einsum("qd,kd->qk", got_rows, keys, preferred_element_type=jnp.float32)
        same = (got_labels[:, None] == labels[None, :]) & (labels[None, :] >= 0)
        same = same & ((index[:, None] != index[None, :]) | (turn > 0))
        terms = jnp.where(same, jnp.exp(20.0 * (cosine - 1.0)), jnp.float32(0.0))
        return (
            lax.ppermute(keys, "member", ring),
            lax.ppermute(labels, "member", ring),
            totals + jnp.sum(terms, axis=1),
        )

    zero = jnp.zeros((slots_dev,), jnp.float32)
    totals = lax.fori_loop(0, members, step, (got_rows, got_labels, zero))[2]
    scores = jnp.log(1.0 + totals)
    back = lax.all_to_all(scores, both, split_axis=0, concat_axis=0, tiled=True)
    return back[slot]


def body(embeddings, cluster, slot):
    send, meta = pack(embeddings, slot, cluster)
    got = partial_sums(send)
    out, flag = pick(got, meta)
    return lax.cond(
        flag[0, 0] > 0.0,
        lambda: general(embeddings, cluster, slot),
        lambda: out.reshape(-1),
    )


def solution(mesh):
    spec = P(("group", "member"))
    in_specs = (P(("group", "member"), None), spec, spec)
    return jax.shard_map(body, mesh=mesh, in_specs=in_specs, out_specs=spec, check_vma=False)
```

time: 275 us -> 73.3 us (0.27)
  waiting for transfers between devices: 133 us -> 0 us
  Pallas kernels: 0 us -> 70.4 us
  blocking collectives: 54 us -> 0 us
  matrix products: 44.4 us -> 0 us
  between operations: 13.5 us -> 0.72 us
  starting transfers between devices: 12.7 us -> 0 us
  other arithmetic: 7.81 us -> 0 us
  local copies, waits for them, and re-layouts: 8.63 us -> 1.77 us
    all_gather x1 -> x0, waiting for transfers between devices: 114 us -> none  [body(): keys = lax.all_gather(got_rows, 'member', axis=0, tiled=True)]
    pallas_call x0 -> x3, Pallas kernels: none -> 70.4 us  [the longest x1 66.1 us: partial_sums(): pl.pallas_call(score_kernel, out_shape=jax.ShapeDtypeStruct((ND, 8, 1, 12...]
    dot_general x1 -> x0, matrix products: 44.4 us -> none  [tile_terms(): jnp.einsum('qd,kd->qk', queries, keys, preferred_element_type=jnp.float32)]
    all_to_all x1 -> x0, blocking collectives: 35.5 us -> none  [body(): lax.all_to_all(send_rows, ('group', 'member'), split_axis=0, concat_axis=...]
    all_to_all x2 -> x0, waiting for transfers between devices: 19.7 us -> none  [the longest x1 9.9 us: body(): lax.all_to_all(send_labels, ('group', 'member'), split_axis=0, concat_axi...]
    all_gather x1 -> x0, blocking collectives: 18.5 us -> none  [body(): key_labels = lax.all_gather(got_labels, 'member', axis=0, tiled=True)]
    all_to_all x2 -> x0, starting transfers between devices: 12.7 us -> none  [the longest x1 7.9 us: body(): lax.all_to_all(scores, ('group', 'member'), split_axis=0, concat_axis=0,...]
    scatter x1 -> x0, other arithmetic: 3.9 us -> none  [body(): send_rows = jnp.zeros((slots_dev, width), jnp.bfloat16).at[slot].set(unit)]
  transfers between devices with their start and end apart: 3 -> 0, of which waited for: 3 -> 0; matrix products, arithmetic and copies ran while one was open for 1% -> 0% of each run, Pallas kernels for 0% -> 0%
where the time goes in v1:
time: 73.3 us; the launch traced here: 73.1 us
  Pallas kernels  70.4 us (96%)
  local copies, waits for them, and re-layouts  1.77 us (2%)
    pallas_call x1, Pallas kernels, partial_sums(): pl.pallas_call(score_kernel, out_shape=jax.ShapeDtypeStruct((ND, 8, 1, 12...  66.1 us
    pallas_call x1, Pallas kernels, pack(): pl.pallas_call(pack_kernel, out_shape=(jax.ShapeDtypeStruct((8, CAPB, D),...  2.91 us
    unnamed x10, local copies, waits for them, and re-layouts  1.77 us

profile of v1, /device:TPU:1, one launch (start us, length us, event | category | flops | bytes accessed | tf_op | source)
XLA Modules:
  0.0 73.1 jit_solution(12683401998475120429)
XLA Ops:
  0.0 0.0 copy-start.3
  0.0 0.0 copy-start.2
  0.0 2.9 %pack.1 = (bf16[8,96,768]{2,1,0:T(8,128)(2,1)S(1)}, s32[2,512]{1,0:T(2,128)S(1)}) custom-call(f32[512,768]{1,0:T(8,128)} %emb_ref.1, s32[1,512]{1,0:T(1,128)} %bitcast.16, s32[1,512]{1,0:T(1,128)} %bitcast.17), custom_call_target="tpu_custom_call" | custom-call | tf_op jit(solution)/shard_map/pack/pallas_call | solution.py:81
  2.9 0.0 copy-start.1
  2.9 0.6 copy-done.1
  3.5 66.1 %scores.1.got_ref = f32[6,8,1,128]{3,2,1,0:T(1,128)S(1)} custom-call(bf16[8,96,768]{2,1,0:T(8,128)(2,1)S(1)} %get-tuple-element.209.send_ref), custom_call_target="tpu_custom_call" | custom-call | tf_op jit(solution)/shard_map/scores/pallas_call | solution.py:334
  69.6 0.0 copy-start
  69.6 0.6 copy-done
  70.2 1.4 %pick.1 = (f32[1,512]{1,0:T(1,128)S(1)}, f32[1,1]{1,0:T(1,128)}) custom-call(f32[6,8,1,128]{3,2,1,0:T(1,128)} %copy-done, s32[2,512]{1,0:T(2,128)} %copy-done.1), custom_call_target="tpu_custom_call" | custom-call | tf_op jit(solution)/shard_map/pick/pallas_call | solution.py:382
  72.3 0.0 copy-done.3
  72.3 0.0 copy-done.2
  72.3 0.2 conditional.1
  72.5 0.0 copy-start.4
  72.5 0.6 copy-done.4
Async XLA Ops:
  0.0 72.3 %copy-start.3 = (s32[512]{0:T(512)S(1)}, s32[512]{0:T(512)}, u32[]{:S(2)}) copy-start(s32[512]{0:T(512)} %param.9) | copy-start | bytes 6148
  0.0 72.3 %copy-start.2 = (f32[512,768]{1,0:T(8,128)S(1)}, f32[512,768]{1,0:T(8,128)}, u32[]{:S(2)}) copy-start(f32[512,768]{1,0:T(8,128)} %emb_ref.1) | copy-start | bytes 4718596
  2.9 0.6 copy-start.1
  69.6 0.6 copy-start
  72.5 0.6 copy-start.4

commit v2 on v0

v2 whole, which is shorter than its diff:
```python
import functools
import math

import jax
import jax.numpy as jnp
from jax import lax
from jax.experimental import pallas as pl
from jax.experimental.pallas import tpu as pltpu
from jax.sharding import PartitionSpec as P

D = 768
CAPB = 96
DOCS = CAPB - 1
NQ = 8
BLK = NQ * CAPB
ND = 6
HALF = BLK // 2
TILE = 256
FLAG_LANE = 127
SCALE = 20.0 * math.log2(math.e)
MESH = pl.DeviceIdType.MESH
HELD = ((0, 0), (1, 0), (3, 0), (2, 0), (0, 1), (0, 2))

def turn(c, q):
    return (c if q % 2 == 0 else 1 - c), (4 - q // 2) % 4


def plan():
    steps = [("route", q) for q in (1, 6, 7, 2, 3, 4, 5)]

    def got(m, *chunks):
        steps.extend(("wait", m, q) for q in chunks)

    def spread(q):
        if q:
            got(0, q)
        steps.extend(("pass", m, 0, q) for m in (4, 1, 2))

    def pass5(*chunks):
        for q in chunks:
            got(4, q)
            steps.append(("pass", 5, 4, q))

    def pass3(*chunks):
        for q in chunks:
            got(1, q)
            got(2, q)
            steps.append(("pass", 3, 1 + q % 2, q))

    def names(m, *halves):
        steps.extend(("names", m, h) for h in halves)

    def product(i, rows, j, cols, both):
        steps.append(("product", i, rows, j, cols, both))

    whole, first, second = (0, BLK), (0, HALF), (HALF, HALF)
    spread(0)
    spread(1)
    pass5(0)
    for q in (2, 3, 6, 7, 4, 5):
        spread(q)
    pass5(1, 2, 3)
    names(0, 0, 1)
    product(0, whole, 0, whole, False)
    pass3(0, 1, 2, 3)
    names(4, 0)
    names(1, 0)
    names(2, 0)
    product(0, whole, 4, first, True)
    product(0, whole, 1, first, True)
    pass5(6, 7)
    product(1, first, 4, first, True)
    product(2, first, 4, first, True)
    pass3(6, 7)
    pass5(4, 5)
    names(4, 1)
    product(0, whole, 4, second, True)
    pass3(4, 5)
    names(1, 1)
    names(2, 1)
    product(0, whole, 1, second, True)
    for m in (1, 2):
        product(m, second, 4, first, True)
        product(m, whole, 4, second, True)
    got(5, 0, 1, 2, 3)
    names(5, 0)
    product(0, whole, 5, first, False)
    product(1, whole, 5, first, True)
    got(3, 0, 1, 2, 3)
    names(3, 0)
    product(0, whole, 3, first, False)
    product(3, first, 4, whole, True)
    product(3, first, 5, first, False)
    got(3, 6, 7, 4, 5)
    names(3, 1)
    product(0, whole, 3, second, False)
    product(3, second, 4, whole, True)
    product(3, second, 5, first, False)
    got(5, 6, 7, 4, 5)
    names(5, 1)
    product(0, whole, 5, second, False)
    product(1, whole, 5, second, True)
    product(3, whole, 5, second, False)
    return steps


def score_kernel(
    emb_ref,
    slot_ref,
    clu_ref,
    out_ref,
    flag_ref,
    send,
    blk,
    lrow,
    lcol,
    rsum,
    csum,
    ret,
    got,
    arr_sem,
    out_sem,
    p1_out,
    ret_in,
    ret_out,
):
    gi = lax.axis_index("group")
    mi = lax.axis_index("member")
    x, c = gi // 2, gi % 2
    z, y = mi // 4, mi % 4

    def line_coord(t):
        return x * (1 - t) + z * t

    def line_dev(t, off, core):
        return (((x + (1 - t) * off) % 4) * 2 + core, ((z + t * off) % 4) * 4 + y)

    def plane_dev(a, b):
        px = (x + c * a) % 4
        pz = (z + (1 - c) * a) % 4
        py = (y + b * (1 + 2 * c)) % 4
        return (px * 2 + c, pz * 4 + py)

    def remote(src, dst, send_sem, recv_sem, dev):
        return pltpu.make_async_remote_copy(
            src_ref=src,
            dst_ref=dst,
            send_sem=send_sem,
            recv_sem=recv_sem,
            device_id=dev,
            device_id_type=MESH,
        )

    def chunk(m, q):
        return blk.at[m, pl.ds(q * CAPB, CAPB), :]

    barrier = pltpu.get_barrier_semaphore()
    partners = [(x * 2 + 1 - c, mi)]
    for off in (1, 2, 3):
        partners += [line_dev(c, off, c), line_dev(1 - c, off, 1 - c), line_dev(c, off, 1 - c)]
    partners += [plane_dev(1, 0), plane_dev(3, 0), plane_dev(0, 1), plane_dev(0, 3)]
    for dev in partners:
        pl.semaphore_signal(barrier, inc=1, device_id=dev, device_id_type=MESH)

    docs = emb_ref.shape[0]
    group = slot_ref[...] // 128
    ids = lax.broadcasted_iota(jnp.int32, (8, docs), 0)
    member = (ids == group).astype(jnp.float32)
    upper = lax.broadcasted_iota(jnp.int32, (docs, docs), 0) < lax.broadcasted_iota(
        jnp.int32, (docs, docs), 1
    )
    before = jnp.dot(
        member.astype(jnp.bfloat16),
        upper.astype(jnp.float32).astype(jnp.bfloat16),
        preferred_element_type=jnp.float32,
    )
    rank = jnp.sum(member * before, axis=0, keepdims=True).astype(jnp.int32)
    fits = rank < DOCS
    place = jnp.where(fits, group * CAPB + rank, -1)

    lane = lax.broadcasted_iota(jnp.int32, (128, docs), 0)
    at_rank = ((lane == rank) & fits).astype(jnp.float32).astype(jnp.bfloat16)
    label = (member * (clu_ref[...] + 1).astype(jnp.float32)).astype(jnp.bfloat16)
    labels = lax.dot_general(
        label, at_rank, (((1,), (1,)), ((), ())), preferred_element_type=jnp.float32
    )
    tile_lane = lax.broadcasted_iota(jnp.int32, (8, 128), 1)
    tile_row = lax.broadcasted_iota(jnp.int32, (8, 128), 0)
    labels = jnp.where(tile_lane == FLAG_LANE, jnp.max(jnp.where(fits, 0.0, 1.0)), labels)

    values = emb_ref[...]
    squares = jnp.sum(values * values, axis=1, keepdims=True)
    unit = (values * lax.rsqrt(squares + 1e-06)).astype(jnp.bfloat16)

    row = lax.broadcasted_iota(jnp.int32, (CAPB, docs), 0)
    last = lax.broadcasted_iota(jnp.int32, (CAPB, 128), 0) == DOCS

    def pack(chunks):
        owners = []
        for q in chunks:
            t, off = turn(c, q)
            owners.append(2 * ((line_coord(t) + off) % 4) + t)
        chosen = jnp.concatenate(
            [(row + g * CAPB == place).astype(jnp.float32) for g in owners], axis=0
        ).astype(jnp.bfloat16)
        packed = jnp.dot(chosen, unit, preferred_element_type=jnp.float32)
        for k, (q, g) in enumerate(zip(chunks, owners)):
            part = packed[k * CAPB : (k + 1) * CAPB]
            tail = jnp.sum(jnp.where(tile_row == g, labels, 0.0), axis=0, keepdims=True)
            part = jnp.concatenate([jnp.where(last, tail, part[:, :128]), part[:, 128:]], axis=1)
            if q:
                send[q] = part.astype(jnp.bfloat16)
            else:
                blk[0, 0:CAPB, :] = part.astype(jnp.bfloat16)

    pack((6, 7, 2, 3))
    pack((4, 5, 1, 0))
    rsum[...] = jnp.zeros_like(rsum)
    csum[...] = jnp.zeros_like(csum)
    pl.semaphore_wait(barrier, len(partners))

    sent = []

    def start(copy):
        copy.start()
        sent.append(copy)

    lanes = lax.broadcasted_iota(jnp.int32, (1, 128), 1)
    overflow = jnp.zeros((1, 128), jnp.float32)
    hops = {1: plane_dev(1, 0), 2: plane_dev(3, 0), 4: plane_dev(0, 1), 5: plane_dev(0, 1)}

    for step in plan():
        if step[0] == "route":
            q = step[1]
            t, off = turn(c, q)
            start(remote(send.at[q], chunk(0, q), p1_out.at[q], arr_sem.at[q], line_dev(t, off, t)))
        elif step[0] == "pass":
            _, m, src, q = step
            start(
                remote(
                    chunk(src, q), chunk(m, q), out_sem.at[(m - 1) * NQ + q],
                    arr_sem.at[m * NQ + q], hops[src if m == 3 else m],
                )
            )
        elif step[0] == "wait":
            _, m, q = step
            pltpu.make_async_copy(chunk(m, q), chunk(m, q), arr_sem.at[m * NQ + q]).wait()
        elif step[0] == "names":
            _, m, h = step
            rows = []
            for q in range(4 * h, 4 * h + 4):
                tail = blk[m, pl.ds(q * CAPB + CAPB - 16, 16), 0:128].astype(jnp.float32)
                rows.append(tail[15:16, :])
            found = jnp.concatenate(rows + [jnp.zeros((4, 128), jnp.float32)], axis=0)
            overflow = jnp.maximum(overflow, jnp.max(found, axis=0, keepdims=True))
            found = jnp.where(lanes < DOCS, found, 0.0)
            wide = jnp.zeros((8, HALF), jnp.float32)
            for k in range(4):
                piece = jnp.concatenate(
                    [
                        jnp.broadcast_to(found[k : k + 1, :], (8, 128)),
                        jnp.zeros((8, HALF - 128), jnp.float32),
                    ],
                    axis=1,
                )
                wide = wide + (pltpu.roll(piece, k * CAPB, axis=1) if k else piece)
            lrow[m, :, h * HALF : (h + 1) * HALF] = wide
            turned = jnp.transpose(
                jnp.concatenate([found, jnp.zeros((120, 128), jnp.float32)], axis=0)
            )
            for k in range(4):
                column = jnp.broadcast_to(turned[0:CAPB, k : k + 1], (CAPB, 128))
                lcol[m, pl.ds(h * HALF + k * CAPB, CAPB), :] = jnp.where(
                    column == 0.0, -1.0, column
                )
        else:
            _, i, (r0, nr), j, (c0, nc), both = step
            tile = TILE if nr % TILE == 0 else nr
            for at in range(r0, r0 + nr, tile):
                cosine = lax.dot_general(
                    blk[i, pl.ds(at, tile), :],
                    blk[j, pl.ds(c0, nc), :],
                    (((1,), (1,)), ((), ())),
                    preferred_element_type=jnp.float32,
                )
                column = lcol[i, pl.ds(at, tile), :]
                total = jnp.zeros((tile, 128), jnp.float32)
                for n in range(nc // 128):
                    part = cosine[:, n * 128 : (n + 1) * 128]
                    here = slice(c0 + n * 128, c0 + (n + 1) * 128)
                    same = column == lrow[j, 0:1, here]
                    if i == j and at < here.stop and here.start < at + tile:
                        mine = at + lax.broadcasted_iota(jnp.int32, (tile, 128), 0)
                        other = here.start + lax.broadcasted_iota(jnp.int32, (tile, 128), 1)
                        same = same & (mine != other)
                    term = jnp.where(same, jnp.exp2(part * SCALE - SCALE), 0.0)
                    total = total + term
                    if both:
                        csum[j, :, here] += jnp.sum(term.reshape(tile // 8, 8, 128), axis=0)
                rsum[i, pl.ds(at, tile), :] += total

    flag = jnp.max(jnp.where(lanes == FLAG_LANE, overflow, 0.0))
    mine = 2 * line_coord(c) + c
    for m in range(ND):
        line = jnp.sum(csum[m], axis=0, keepdims=True)
        if m < 4:
            line = line + jnp.sum(jnp.transpose(rsum[m]), axis=0, keepdims=True)
        line = jnp.broadcast_to(line, (8, BLK))
        for q in range(NQ):
            piece = (pltpu.roll(line, BLK - q * CAPB, axis=1) if q else line)[0:1, 0:128]
            ret[m, q] = jnp.where(lanes == FLAG_LANE, flag, piece)
    for m in range(ND):
        a, b = HELD[m]
        for q in range(NQ):
            if m == 0 and q == 0:
                pltpu.make_async_copy(ret.at[0, 0], got.at[0, mine], ret_in).start()
                continue
            dl, cs = q // 2, q % 2
            core = c if cs == 0 else 1 - c
            px = (x + c * (4 - a) + (1 - c) * dl) % 4
            pz = (z + (1 - c) * (4 - a) + c * dl) % 4
            py = (y + (4 - b) * (1 + 2 * c)) % 4
            remote(
                ret.at[m, q], got.at[m, mine], ret_out, ret_in, (px * 2 + core, pz * 4 + py)
            ).start()
    pltpu.make_async_copy(got, got, ret_in).wait()

    total = got[0, :, 0, :]
    for m in range(1, ND):
        total = total + got[m, :, 0, :]
    flag_ref[...] = jnp.max(jnp.where(tile_lane == FLAG_LANE, total, 0.0), keepdims=True)
    scores = jnp.log(1.0 + total)
    for n in range(docs // 128):
        here = slice(n * 128, (n + 1) * 128)
        spot = jnp.broadcast_to(jnp.minimum(rank[:, here], 127), (8, 128))
        picked = jnp.take_along_axis(scores, spot, axis=1)
        out_ref[:, here] = jnp.sum(
            jnp.where(tile_row == group[:, here], picked, 0.0), axis=0, keepdims=True
        )

    for copy in sent:
        copy.wait_send()
    most = ret.at[0, pl.ds(1, NQ - 1)]
    pltpu.make_async_copy(most, most, ret_out).wait()
    rest = ret.at[pl.ds(1, ND - 1)]
    pltpu.make_async_copy(rest, rest, ret_out).wait()


def fast(embeddings, cluster, slot):
    rows = embeddings.shape[0]
    dma = pltpu.SemaphoreType.DMA
    vmem = pl.BlockSpec(memory_space=pltpu.VMEM)
    return pl.pallas_call(
        score_kernel,
        out_shape=(
            jax.ShapeDtypeStruct((1, rows), jnp.float32),
            jax.ShapeDtypeStruct((1, 1), jnp.float32),
        ),
        in_specs=[vmem] * 3,
        out_specs=(vmem,) * 2,
        scratch_shapes=[
            pltpu.VMEM((NQ, CAPB, D), jnp.bfloat16),
            pltpu.VMEM((ND, BLK, D), jnp.bfloat16),
            pltpu.VMEM((ND, 8, BLK), jnp.float32),
            pltpu.VMEM((ND, BLK, 128), jnp.float32),
            pltpu.VMEM((4, BLK, 128), jnp.float32),
            pltpu.VMEM((ND, 8, BLK), jnp.float32),
            pltpu.VMEM((ND, NQ, 1, 128), jnp.float32),
            pltpu.VMEM((ND, 8, 1, 128), jnp.float32),
            dma((ND * NQ,)),
            dma(((ND - 1) * NQ,)),
            dma((NQ,)),
            dma(()),
            dma(()),
        ],
        compiler_params=pltpu.CompilerParams(
            collective_id=0, has_side_effects=True, vmem_limit_bytes=48 << 20
        ),
        name="scores",
    )(embeddings, slot.reshape(1, rows), cluster.reshape(1, rows))


def general(embeddings, cluster, slot):
    rows, width = embeddings.shape
    slots_dev = 2 * rows
    unit = (
        embeddings * lax.rsqrt(jnp.sum(embeddings * embeddings, axis=1, keepdims=True) + 1e-06)
    ).astype(jnp.bfloat16)
    both = ("group", "member")
    send_rows = jnp.zeros((slots_dev, width), jnp.bfloat16).at[slot].set(unit)
    send_labels = jnp.full((slots_dev,), -1, jnp.int32).at[slot].set(cluster)
    got_rows = lax.all_to_all(send_rows, both, split_axis=0, concat_axis=0, tiled=True)
    got_labels = lax.all_to_all(send_labels, both, split_axis=0, concat_axis=0, tiled=True)
    members = lax.axis_size("member")
    ring = [(i, (i + 1) % members) for i in range(members)]
    index = jnp.arange(slots_dev, dtype=jnp.int32)

    def step(turn, state):
        keys, labels, totals = state
        cosine = jnp.einsum("qd,kd->qk", got_rows, keys, preferred_element_type=jnp.float32)
        same = (got_labels[:, None] == labels[None, :]) & (labels[None, :] >= 0)
        same = same & ((index[:, None] != index[None, :]) | (turn > 0))
        terms = jnp.where(same, jnp.exp(20.0 * (cosine - 1.0)), jnp.float32(0.0))
        return (
            lax.ppermute(keys, "member", ring),
            lax.ppermute(labels, "member", ring),
            totals + jnp.sum(terms, axis=1),
        )

    zero = jnp.zeros((slots_dev,), jnp.float32)
    totals = lax.fori_loop(0, members, step, (got_rows, got_labels, zero))[2]
    scores = jnp.log(1.0 + totals)
    back = lax.all_to_all(scores, both, split_axis=0, concat_axis=0, tiled=True)
    return back[slot]


def body(embeddings, cluster, slot):
    out, flag = fast(embeddings, cluster, slot)
    return lax.cond(
        flag[0, 0] > 0.0,
        lambda: general(embeddings, cluster, slot),
        lambda: out.reshape(-1),
    )


def solution(mesh):
    spec = P(("group", "member"))
    in_specs = (P(("group", "member"), None), spec, spec)
    return jax.shard_map(body, mesh=mesh, in_specs=in_specs, out_specs=spec, check_vma=False)
```

time: 275 us -> 52.2 us (0.19)
  waiting for transfers between devices: 133 us -> 0 us
  blocking collectives: 54 us -> 0 us
  Pallas kernels: 0 us -> 50.7 us
  matrix products: 44.4 us -> 0 us
  between operations: 13.5 us -> 0.72 us
  starting transfers between devices: 12.7 us -> 0 us
  local copies, waits for them, and re-layouts: 8.63 us -> 0.59 us
  other arithmetic: 7.81 us -> 0 us
    all_gather x1 -> x0, waiting for transfers between devices: 114 us -> none  [body(): keys = lax.all_gather(got_rows, 'member', axis=0, tiled=True)]
    pallas_call x0 -> x1, Pallas kernels: none -> 50.7 us  [fast(): pl.pallas_call(score_kernel, out_shape=(jax.ShapeDtypeStruct((1, rows), j...]
    dot_general x1 -> x0, matrix products: 44.4 us -> none  [tile_terms(): jnp.einsum('qd,kd->qk', queries, keys, preferred_element_type=jnp.float32)]
    all_to_all x1 -> x0, blocking collectives: 35.5 us -> none  [body(): lax.all_to_all(send_rows, ('group', 'member'), split_axis=0, concat_axis=...]
    all_to_all x2 -> x0, waiting for transfers between devices: 19.7 us -> none  [the longest x1 9.9 us: body(): lax.all_to_all(send_labels, ('group', 'member'), split_axis=0, concat_axi...]
    all_gather x1 -> x0, blocking collectives: 18.5 us -> none  [body(): key_labels = lax.all_gather(got_labels, 'member', axis=0, tiled=True)]
    all_to_all x2 -> x0, starting transfers between devices: 12.7 us -> none  [the longest x1 7.9 us: body(): lax.all_to_all(scores, ('group', 'member'), split_axis=0, concat_axis=0,...]
    scatter x1 -> x0, other arithmetic: 3.9 us -> none  [body(): send_rows = jnp.zeros((slots_dev, width), jnp.bfloat16).at[slot].set(unit)]
  transfers between devices with their start and end apart: 3 -> 0, of which waited for: 3 -> 0; matrix products, arithmetic and copies ran while one was open for 1% -> 0% of each run, Pallas kernels for 0% -> 0%
where the time goes in v2:
time: 52.2 us; the launch traced here: 52 us
  Pallas kernels  50.7 us (97%)
  between operations  0.72 us (1%)
  local copies, waits for them, and re-layouts  0.59 us (1%)
    pallas_call x1, Pallas kernels, fast(): pl.pallas_call(score_kernel, out_shape=(jax.ShapeDtypeStruct((1, rows), j...  50.7 us

profile of v2, /device:TPU:1, one launch (start us, length us, event | category | flops | bytes accessed | tf_op | source)
XLA Modules:
  0.0 52.0 jit_solution(758573687455755282)
XLA Ops:
  0.0 0.0 copy-start.1
  0.0 0.0 copy-start
  0.0 50.7 %scores.1 = (f32[1,512]{1,0:T(1,128)S(1)}, f32[1,1]{1,0:T(1,128)}) custom-call(f32[512,768]{1,0:T(8,128)} %emb_ref.1, s32[1,512]{1,0:T(1,128)} %bitcast.16, s32[1,512]{1,0:T(1,128)} %bitcast.17), custom_call_target="tpu_custom_call" | custom-call | tf_op jit(solution)/shard_map/scores/pallas_call | solution.py:353
  51.4 0.0 copy-done.1
  51.4 0.0 copy-done
  51.5 0.6 %copy.23 = f32[512]{0:T(512)} copy(f32[512]{0:T(512)S(1)} %get-tuple-element.209) | data formatting | bytes 4096
  (1 shorter events, 0.0 us)
Async XLA Ops:
  0.0 51.4 %copy-start.1 = (s32[512]{0:T(512)S(1)}, s32[512]{0:T(512)}, u32[]{:S(2)}) copy-start(s32[512]{0:T(512)} %param.9) | copy-start | bytes 6148
  0.0 51.4 %copy-start = (f32[512,768]{1,0:T(8,128)S(1)}, f32[512,768]{1,0:T(8,128)}, u32[]{:S(2)}) copy-start(f32[512,768]{1,0:T(8,128)} %emb_ref.1) | copy-start | bytes 4718596

commit v3 on v2

--- a/solution.py
+++ b/solution.py
@@ -26,7 +26,7 @@
 
 
 def plan():
-    steps = [("route", q) for q in (1, 6, 7, 2, 3, 4, 5)]
+    steps = []
 
     def got(m, *chunks):
         steps.extend(("wait", m, q) for q in chunks)
@@ -50,57 +50,65 @@
     def names(m, *halves):
         steps.extend(("names", m, h) for h in halves)
 
-    def product(i, rows, j, cols, both):
-        steps.append(("product", i, rows, j, cols, both))
+    def product(i, rows, j, cols, sums):
+        steps.append(("product", i, rows, j, cols, sums))
 
     whole, first, second = (0, BLK), (0, HALF), (HALF, HALF)
+    steps.append(("pack", (2, 3, 1, 0)))
+    steps.append(("meet",))
+    steps.extend(("route", q) for q in (1, 2, 3))
     spread(0)
+    steps.append(("pack", (6, 7, 4, 5)))
+    steps.extend(("route", q) for q in (6, 7, 4, 5))
     spread(1)
     pass5(0)
     for q in (2, 3, 6, 7, 4, 5):
         spread(q)
     pass5(1, 2, 3)
     names(0, 0, 1)
-    product(0, whole, 0, whole, False)
+    product(0, whole, 0, whole, "rows")
     pass3(0, 1, 2, 3)
     names(4, 0)
     names(1, 0)
     names(2, 0)
-    product(0, whole, 4, first, True)
-    product(0, whole, 1, first, True)
+    product(0, whole, 4, first, "both")
+    product(0, whole, 1, first, "both")
     pass5(6, 7)
-    product(1, first, 4, first, True)
-    product(2, first, 4, first, True)
+    product(1, first, 4, first, "both")
+    product(2, first, 4, first, "both")
     pass3(6, 7)
     pass5(4, 5)
     names(4, 1)
-    product(0, whole, 4, second, True)
+    product(0, whole, 4, second, "both")
     pass3(4, 5)
     names(1, 1)
     names(2, 1)
-    product(0, whole, 1, second, True)
-    for m in (1, 2):
-        product(m, second, 4, first, True)
-        product(m, whole, 4, second, True)
+    product(0, whole, 1, second, "both")
+    for m in (2, 1):
+        product(m, second, 4, first, "both")
+        product(m, whole, 4, second, "both")
+    steps.append(("return", ((2, range(NQ)),)))
     got(5, 0, 1, 2, 3)
     names(5, 0)
-    product(0, whole, 5, first, False)
-    product(1, whole, 5, first, True)
+    product(0, whole, 5, first, "rows")
+    product(1, whole, 5, first, "both")
     got(3, 0, 1, 2, 3)
     names(3, 0)
-    product(0, whole, 3, first, False)
-    product(3, first, 4, whole, True)
-    product(3, first, 5, first, False)
+    product(0, whole, 3, first, "rows")
+    product(3, first, 4, whole, "both")
+    product(3, first, 5, first, "rows")
     got(3, 6, 7, 4, 5)
     names(3, 1)
-    product(0, whole, 3, second, False)
-    product(3, second, 4, whole, True)
-    product(3, second, 5, first, False)
+    product(0, whole, 3, second, "rows")
+    product(3, second, 4, whole, "both")
+    product(3, second, 5, first, "cols")
+    steps.append(("return", ((3, range(NQ)), (4, range(NQ)), (5, range(4)))))
     got(5, 6, 7, 4, 5)
     names(5, 1)
-    product(0, whole, 5, second, False)
-    product(1, whole, 5, second, True)
-    product(3, whole, 5, second, False)
+    product(0, whole, 5, second, "rows")
+    product(1, whole, 5, second, "both")
+    product(3, whole, 5, second, "cols")
+    steps.append(("return", ((5, range(4, NQ)), (1, range(NQ)), (0, range(NQ)))))
     return steps
 
 
@@ -110,6 +118,8 @@
     clu_ref,
     out_ref,
     flag_ref,
+    held,
+    unit,
     send,
     blk,
     lrow,
@@ -118,6 +128,7 @@
     csum,
     ret,
     got,
+    emb_sem,
     arr_sem,
     out_sem,
     p1_out,
@@ -163,6 +174,13 @@
         pl.semaphore_signal(barrier, inc=1, device_id=dev, device_id_type=MESH)
 
     docs = emb_ref.shape[0]
+    step_rows = docs // 4
+    loads = []
+    for k in range(4):
+        rows = pl.ds(k * step_rows, step_rows)
+        loads.append(pltpu.make_async_copy(emb_ref.at[rows], held.at[rows], emb_sem.at[k]))
+        loads[k].start()
+
     group = slot_ref[...] // 128
     ids = lax.broadcasted_iota(jnp.int32, (8, docs), 0)
     member = (ids == group).astype(jnp.float32)
@@ -188,9 +206,14 @@
     tile_row = lax.broadcasted_iota(jnp.int32, (8, 128), 0)
     labels = jnp.where(tile_lane == FLAG_LANE, jnp.max(jnp.where(fits, 0.0, 1.0)), labels)
 
-    values = emb_ref[...]
-    squares = jnp.sum(values * values, axis=1, keepdims=True)
-    unit = (values * lax.rsqrt(squares + 1e-06)).astype(jnp.bfloat16)
+    rsum[...] = jnp.zeros_like(rsum)
+    csum[...] = jnp.zeros_like(csum)
+    for k in range(4):
+        rows = pl.ds(k * step_rows, step_rows)
+        loads[k].wait()
+        values = held[rows, :]
+        squares = jnp.sum(values * values, axis=1, keepdims=True)
+        unit[rows, :] = (values * lax.rsqrt(squares + 1e-06)).astype(jnp.bfloat16)
 
     row = lax.broadcasted_iota(jnp.int32, (CAPB, docs), 0)
     last = lax.broadcasted_iota(jnp.int32, (CAPB, 128), 0) == DOCS
@@ -203,7 +226,7 @@
         chosen = jnp.concatenate(
             [(row + g * CAPB == place).astype(jnp.float32) for g in owners], axis=0
         ).astype(jnp.bfloat16)
-        packed = jnp.dot(chosen, unit, preferred_element_type=jnp.float32)
+        packed = jnp.dot(chosen, unit[...], preferred_element_type=jnp.float32)
         for k, (q, g) in enumerate(zip(chunks, owners)):
             part = packed[k * CAPB : (k + 1) * CAPB]
             tail = jnp.sum(jnp.where(tile_row == g, labels, 0.0), axis=0, keepdims=True)
@@ -213,12 +236,6 @@
             else:
                 blk[0, 0:CAPB, :] = part.astype(jnp.bfloat16)
 
-    pack((6, 7, 2, 3))
-    pack((4, 5, 1, 0))
-    rsum[...] = jnp.zeros_like(rsum)
-    csum[...] = jnp.zeros_like(csum)
-    pl.semaphore_wait(barrier, len(partners))
-
     sent = []
 
     def start(copy):
@@ -229,8 +246,41 @@
     overflow = jnp.zeros((1, 128), jnp.float32)
     hops = {1: plane_dev(1, 0), 2: plane_dev(3, 0), 4: plane_dev(0, 1), 5: plane_dev(0, 1)}
 
+    home = 2 * line_coord(c) + c
+
+    def give_back(blocks, seen):
+        flag = jnp.max(jnp.where(lanes == FLAG_LANE, seen, 0.0))
+        for m, chunks in blocks:
+            line = jnp.sum(csum[m], axis=0, keepdims=True)
+            if m < 4:
+                line = line + jnp.sum(jnp.transpose(rsum[m]), axis=0, keepdims=True)
+            line = jnp.broadcast_to(line, (8, BLK))
+            for q in chunks:
+                piece = (pltpu.roll(line, BLK - q * CAPB, axis=1) if q else line)[0:1, 0:128]
+                ret[m, q] = jnp.where(lanes == FLAG_LANE, flag, piece)
+        for m, chunks in blocks:
+            a, b = HELD[m]
+            for q in chunks:
+                if m == 0 and q == 0:
+                    pltpu.make_async_copy(ret.at[0, 0], got.at[0, home], ret_in).start()
+                    continue
+                dl, cs = q // 2, q % 2
+                core = c if cs == 0 else 1 - c
+                px = (x + c * (4 - a) + (1 - c) * dl) % 4
+                pz = (z + (1 - c) * (4 - a) + c * dl) % 4
+                py = (y + (4 - b) * (1 + 2 * c)) % 4
+                remote(
+                    ret.at[m, q], got.at[m, home], ret_out, ret_in, (px * 2 + core, pz * 4 + py)
+                ).start()
+
     for step in plan():
-        if step[0] == "route":
+        if step[0] == "pack":
+            pack(step[1])
+        elif step[0] == "meet":
+            pl.semaphore_wait(barrier, len(partners))
+        elif step[0] == "return":
+            give_back(step[1], overflow)
+        elif step[0] == "route":
             q = step[1]
             t, off = turn(c, q)
             start(remote(send.at[q], chunk(0, q), p1_out.at[q], arr_sem.at[q], line_dev(t, off, t)))
@@ -274,7 +324,7 @@
                     column == 0.0, -1.0, column
                 )
         else:
-            _, i, (r0, nr), j, (c0, nc), both = step
+            _, i, (r0, nr), j, (c0, nc), sums = step
             tile = TILE if nr % TILE == 0 else nr
             for at in range(r0, r0 + nr, tile):
                 cosine = lax.dot_general(
@@ -294,35 +344,13 @@
                         other = here.start + lax.broadcasted_iota(jnp.int32, (tile, 128), 1)
                         same = same & (mine != other)
                     term = jnp.where(same, jnp.exp2(part * SCALE - SCALE), 0.0)
-                    total = total + term
-                    if both:
+                    if sums != "cols":
+                        total = total + term
+                    if sums != "rows":
                         csum[j, :, here] += jnp.sum(term.reshape(tile // 8, 8, 128), axis=0)
-                rsum[i, pl.ds(at, tile), :] += total
-
-    flag = jnp.max(jnp.where(lanes == FLAG_LANE, overflow, 0.0))
-    mine = 2 * line_coord(c) + c
-    for m in range(ND):
-        line = jnp.sum(csum[m], axis=0, keepdims=True)
-        if m < 4:
-            line = line + jnp.sum(jnp.transpose(rsum[m]), axis=0, keepdims=True)
-        line = jnp.broadcast_to(line, (8, BLK))
-        for q in range(NQ):
-            piece = (pltpu.roll(line, BLK - q * CAPB, axis=1) if q else line)[0:1, 0:128]
-            ret[m, q] = jnp.where(lanes == FLAG_LANE, flag, piece)
-    for m in range(ND):
-        a, b = HELD[m]
-        for q in range(NQ):
-            if m == 0 and q == 0:
-                pltpu.make_async_copy(ret.at[0, 0], got.at[0, mine], ret_in).start()
-                continue
-            dl, cs = q // 2, q % 2
-            core = c if cs == 0 else 1 - c
-            px = (x + c * (4 - a) + (1 - c) * dl) % 4
-            pz = (z + (1 - c) * (4 - a) + c * dl) % 4
-            py = (y + (4 - b) * (1 + 2 * c)) % 4
-            remote(
-                ret.at[m, q], got.at[m, mine], ret_out, ret_in, (px * 2 + core, pz * 4 + py)
-            ).start()
+                if sums != "cols":
+                    rsum[i, pl.ds(at, tile), :] += total
+
     pltpu.make_async_copy(got, got, ret_in).wait()
 
     total = got[0, :, 0, :]
@@ -356,9 +384,11 @@
             jax.ShapeDtypeStruct((1, rows), jnp.float32),
             jax.ShapeDtypeStruct((1, 1), jnp.float32),
         ),
-        in_specs=[vmem] * 3,
+        in_specs=[pl.BlockSpec(memory_space=pl.ANY), vmem, vmem],
         out_specs=(vmem,) * 2,
         scratch_shapes=[
+            pltpu.VMEM((rows, D), jnp.float32),
+            pltpu.VMEM((rows, D), jnp.bfloat16),
             pltpu.VMEM((NQ, CAPB, D), jnp.bfloat16),
             pltpu.VMEM((ND, BLK, D), jnp.bfloat16),
             pltpu.VMEM((ND, 8, BLK), jnp.float32),
@@ -367,6 +397,7 @@
             pltpu.VMEM((ND, 8, BLK), jnp.float32),
             pltpu.VMEM((ND, NQ, 1, 128), jnp.float32),
             pltpu.VMEM((ND, 8, 1, 128), jnp.float32),
+            dma((4,)),
             dma((ND * NQ,)),
             dma(((ND - 1) * NQ,)),
             dma((NQ,)),

time: 52.2 us -> 49 us (0.939)
  Pallas kernels: 50.7 us -> 47.5 us
    pallas_call x1, Pallas kernels: 50.7 us -> 47.5 us  [fast(): pl.pallas_call(score_kernel, out_shape=(jax.ShapeDtypeStruct((1, rows), j...]
where the time goes in v3:
time: 49 us; the launch traced here: 48.8 us
  Pallas kernels  47.5 us (97%)
  between operations  0.72 us (1%)
  local copies, waits for them, and re-layouts  0.59 us (1%)
    pallas_call x1, Pallas kernels, fast(): pl.pallas_call(score_kernel, out_shape=(jax.ShapeDtypeStruct((1, rows), j...  47.5 us

profile of v3, /device:TPU:1, one launch (start us, length us, event | category | flops | bytes accessed | tf_op | source)
XLA Modules:
  0.0 48.8 jit_solution(17282602572971845041)
XLA Ops:
  0.0 0.0 copy-start.1
  0.0 0.0 copy-start
  0.0 47.5 %scores.1 = (f32[1,512]{1,0:T(1,128)S(1)}, f32[1,1]{1,0:T(1,128)}) custom-call(f32[512,768]{1,0:T(8,128)} %emb_ref.1, s32[1,512]{1,0:T(1,128)} %bitcast.16, s32[1,512]{1,0:T(1,128)} %bitcast.17), custom_call_target="tpu_custom_call" | custom-call | tf_op jit(solution)/shard_map/scores/pallas_call | solution.py:381
  48.2 0.0 copy-done.1
  48.2 0.0 copy-done
  48.2 0.6 %copy.23 = f32[512]{0:T(512)} copy(f32[512]{0:T(512)S(1)} %get-tuple-element.209) | data formatting | bytes 4096
  (1 shorter events, 0.0 us)
Async XLA Ops:
  0.0 48.2 %copy-start.1 = (s32[512]{0:T(512)S(1)}, s32[512]{0:T(512)}, u32[]{:S(2)}) copy-start(s32[512]{0:T(512)} %param.9) | copy-start | bytes 6148
  0.0 48.2 %copy-start = (f32[512,768]{1,0:T(8,128)S(1)}, f32[512,768]{1,0:T(8,128)}, u32[]{:S(2)}) copy-start(f32[512,768]{1,0:T(8,128)} %emb_ref.1) | copy-start | bytes 4718596

commit v4 on v3

--- a/solution.py
+++ b/solution.py
@@ -423,23 +423,22 @@
     got_rows = lax.all_to_all(send_rows, both, split_axis=0, concat_axis=0, tiled=True)
     got_labels = lax.all_to_all(send_labels, both, split_axis=0, concat_axis=0, tiled=True)
     members = lax.axis_size("member")
-    ring = [(i, (i + 1) % members) for i in range(members)]
+    me = lax.axis_index("member")
+    everyone = jnp.broadcast_to(got_rows[None], (members, slots_dev, width))
+    keys = lax.all_to_all(everyone, "member", split_axis=0, concat_axis=0)
+    names = jnp.broadcast_to(got_labels[None], (members, slots_dev))
+    key_labels = lax.all_to_all(names, "member", split_axis=0, concat_axis=0)
     index = jnp.arange(slots_dev, dtype=jnp.int32)
 
-    def step(turn, state):
-        keys, labels, totals = state
-        cosine = jnp.einsum("qd,kd->qk", got_rows, keys, preferred_element_type=jnp.float32)
+    def step(k, totals):
+        cosine = jnp.einsum("qd,kd->qk", got_rows, keys[k], preferred_element_type=jnp.float32)
+        labels = key_labels[k]
         same = (got_labels[:, None] == labels[None, :]) & (labels[None, :] >= 0)
-        same = same & ((index[:, None] != index[None, :]) | (turn > 0))
+        same = same & (me * slots_dev + index[:, None] != k * slots_dev + index[None, :])
         terms = jnp.where(same, jnp.exp(20.0 * (cosine - 1.0)), jnp.float32(0.0))
-        return (
-            lax.ppermute(keys, "member", ring),
-            lax.ppermute(labels, "member", ring),
-            totals + jnp.sum(terms, axis=1),
-        )
-
-    zero = jnp.zeros((slots_dev,), jnp.float32)
-    totals = lax.fori_loop(0, members, step, (got_rows, got_labels, zero))[2]
+        return totals + jnp.sum(terms, axis=1)
+
+    totals = lax.fori_loop(0, members, step, jnp.zeros((slots_dev,), jnp.float32))
     scores = jnp.log(1.0 + totals)
     back = lax.all_to_all(scores, both, split_axis=0, concat_axis=0, tiled=True)
     return back[slot]

time: 49 us -> 49 us (level)
  no operation moved by 1% of the time
where the time goes in v4:
time: 49 us; the launch traced here: 48.8 us
  Pallas kernels  47.5 us (97%)
  between operations  0.72 us (1%)
  local copies, waits for them, and re-layouts  0.59 us (1%)
    pallas_call x1, Pallas kernels, fast(): pl.pallas_call(score_kernel, out_shape=(jax.ShapeDtypeStruct((1, rows), j...  47.5 us

profile of v4, /device:TPU:1, one launch (start us, length us, event | category | flops | bytes accessed | tf_op | source)
XLA Modules:
  0.0 48.8 jit_solution(11833197451969129438)
XLA Ops:
  0.0 0.0 copy-start.1
  0.0 0.0 copy-start
  0.0 47.5 %scores.1 = (f32[1,512]{1,0:T(1,128)S(1)}, f32[1,1]{1,0:T(1,128)}) custom-call(f32[512,768]{1,0:T(8,128)} %emb_ref.1, s32[1,512]{1,0:T(1,128)} %bitcast.35, s32[1,512]{1,0:T(1,128)} %bitcast.36), custom_call_target="tpu_custom_call" | custom-call | tf_op jit(solution)/shard_map/scores/pallas_call | solution.py:381
  48.2 0.0 copy-done.1
  48.2 0.0 copy-done
  48.2 0.6 %copy.20 = f32[512]{0:T(512)} copy(f32[512]{0:T(512)S(1)} %get-tuple-element.225) | data formatting | bytes 4096
  (1 shorter events, 0.0 us)
Async XLA Ops:
  0.0 48.2 %copy-start.1 = (s32[512]{0:T(512)S(1)}, s32[512]{0:T(512)}, u32[]{:S(2)}) copy-start(s32[512]{0:T(512)} %param.9) | copy-start | bytes 6148
  0.0 48.2 %copy-start = (f32[512,768]{1,0:T(8,128)S(1)}, f32[512,768]{1,0:T(8,128)}, u32[]{:S(2)}) copy-start(f32[512,768]{1,0:T(8,128)} %emb_ref.1) | copy-start | bytes 4718596

commit v5 on v4

--- a/solution.py
+++ b/solution.py
@@ -74,8 +74,6 @@
     product(0, whole, 4, first, "both")
     product(0, whole, 1, first, "both")
     pass5(6, 7)
-    product(1, first, 4, first, "both")
-    product(2, first, 4, first, "both")
     pass3(6, 7)
     pass5(4, 5)
     names(4, 1)
@@ -83,10 +81,9 @@
     pass3(4, 5)
     names(1, 1)
     names(2, 1)
+    product(2, whole, 4, whole, "both")
+    product(1, whole, 4, whole, "both")
     product(0, whole, 1, second, "both")
-    for m in (2, 1):
-        product(m, second, 4, first, "both")
-        product(m, whole, 4, second, "both")
     steps.append(("return", ((2, range(NQ)),)))
     got(5, 0, 1, 2, 3)
     names(5, 0)

time: 49 us -> 49 us (level)
  no operation moved by 1% of the time
where the time goes in v5:
time: 49 us; the launch traced here: 48.8 us
  Pallas kernels  47.5 us (97%)
  between operations  0.72 us (1%)
  local copies, waits for them, and re-layouts  0.59 us (1%)
    pallas_call x1, Pallas kernels, fast(): pl.pallas_call(score_kernel, out_shape=(jax.ShapeDtypeStruct((1, rows), j...  47.5 us

profile of v5, /device:TPU:1, one launch (start us, length us, event | category | flops | bytes accessed | tf_op | source)
XLA Modules:
  0.0 48.8 jit_solution(903932163657764850)
XLA Ops:
  0.0 0.0 copy-start.1
  0.0 0.0 copy-start
  0.0 47.5 %scores.1 = (f32[1,512]{1,0:T(1,128)S(1)}, f32[1,1]{1,0:T(1,128)}) custom-call(f32[512,768]{1,0:T(8,128)} %emb_ref.1, s32[1,512]{1,0:T(1,128)} %bitcast.35, s32[1,512]{1,0:T(1,128)} %bitcast.36), custom_call_target="tpu_custom_call" | custom-call | tf_op jit(solution)/shard_map/scores/pallas_call | solution.py:378
  48.2 0.0 copy-done.1
  48.2 0.0 copy-done
  48.2 0.6 %copy.20 = f32[512]{0:T(512)} copy(f32[512]{0:T(512)S(1)} %get-tuple-element.225) | data formatting | bytes 4096
  (1 shorter events, 0.0 us)
Async XLA Ops:
  0.0 48.2 %copy-start.1 = (s32[512]{0:T(512)S(1)}, s32[512]{0:T(512)}, u32[]{:S(2)}) copy-start(s32[512]{0:T(512)} %param.9) | copy-start | bytes 6148
  0.0 48.2 %copy-start = (f32[512,768]{1,0:T(8,128)S(1)}, f32[512,768]{1,0:T(8,128)}, u32[]{:S(2)}) copy-start(f32[512,768]{1,0:T(8,128)} %emb_ref.1) | copy-start | bytes 4718596
